TPU v7x, 32 devices: a whole 2x2x4 slice. The times are simulated.
32 devices in a mesh: visit: 4 (over z), patch: 8 (over y, x, core).
Axes of the slice: x: 2, y: 2, z: 4, core: 2. Of those that a mesh axis runs over, the one named last changes fastest.
Arguments:
- warped_tiles: bfloat16 [1024, 256, 256], P(('visit', 'patch')), may hold values from -6 to 6
- tile_weights: bfloat16 [1024], P(('visit', 'patch')), may hold values from 1 to 9984
- kernel_taps: bfloat16 [1024, 2, 15], P(('visit', 'patch')), may hold values from -3 to 3
- patch_routes: int32 [1024, 1], P(('visit', 'patch')), may hold values from 0 to 7; in each aligned block of 32 rows (0 to 31, 32 to 63, ...) at most 8 rows name the same one
Outputs:
- difference: bfloat16 [1024, 256, 256], P(('visit', 'patch'))
- coadd_image: bfloat16 [8, 256, 256], P('patch')
Inputs may be any that keep to these rules, and one draw needn't show every extreme that they name: `patch_routes`: among the 32 rows of one device no patch is named more than 8 times, a bound that some block reaches; every patch is named by some row.
All inputs are finite; a program needn't handle non-finite values.
Results may differ from a plain program's by a relative error of at most 0.0046.
Values may be sent and summed in bfloat16 or wider, within the bound.
A program may use at most 128 MiB of HBM per device.

v0:
```python
import functools
import jax
import jax.numpy as jnp
from jax import lax
from jax.experimental import pallas as pl
from jax.experimental.pallas import tpu as pltpu
from jax.sharding import PartitionSpec as P


def sum_kernel(patches, routes, weights, tiles, part, totals, acc):
    acc[...] = jnp.zeros_like(acc)
    for t in range(tiles.shape[0]):
        acc[routes[t]] += tiles[t].astype(jnp.float32) * weights[t]
    part[...] = acc[...].astype(part.dtype)

    @pl.when(pl.program_id(0) == 0)
    def _():
        totals[...] = jnp.zeros_like(totals)
        for t in range(tiles.shape[0]):
            totals[routes[t]] += jnp.full(totals.shape[1:], weights[t], jnp.float32)


def local_sums(tiles, weights, routes, patches, chunk, dtype):
    count, side, _ = tiles.shape
    return pl.pallas_call(
        functools.partial(sum_kernel, patches),
        grid_spec=pltpu.PrefetchScalarGridSpec(
            num_scalar_prefetch=2,
            grid=(side // chunk,),
            in_specs=[pl.BlockSpec((count, chunk, side), lambda i, *_: (0, i, 0))],
            out_specs=[
                pl.BlockSpec((patches, chunk, side), lambda i, *_: (0, i, 0)),
                pl.BlockSpec((patches, 8, 128), lambda i, *_: (0, 0, 0)),
            ],
            scratch_shapes=[pltpu.VMEM((patches, chunk, side), jnp.float32)],
        ),
        out_shape=[
            jax.ShapeDtypeStruct((patches, side, side), dtype),
            jax.ShapeDtypeStruct((patches, 8, 128), jnp.float32),
        ],
        name="local_sums",
    )(routes, weights, tiles)


def band(row):
    half = 128
    ring = pltpu.roll(jnp.broadcast_to(row, (half, half)), 0, 1, stride=1, stride_axis=0)
    gap = lax.broadcasted_iota(jnp.int32, (half, half), 1) - lax.broadcasted_iota(jnp.int32, (half, half), 0)
    zero = jnp.zeros_like(ring)
    near = jnp.where((gap < 64) & (gap > -64), ring, zero).astype(jnp.bfloat16)
    upper = jnp.where(gap <= -64, ring, zero).astype(jnp.bfloat16)
    lower = jnp.where(gap >= 64, ring, zero).astype(jnp.bfloat16)
    return jnp.concatenate(
        [jnp.concatenate([near, upper], axis=1), jnp.concatenate([lower, near], axis=1)], axis=0
    )


def match_kernel(routes, taps, tiles, coadd, out):
    step = pl.program_id(0)
    group = tiles.shape[0]
    for g in range(group):
        image = coadd[routes[step * group + g]]
        row_pass = jnp.dot(band(taps[g, 0:1, :]), image, preferred_element_type=jnp.float32).astype(jnp.bfloat16)
        template = jnp.dot(row_pass, band(taps[g, 1:2, :]), preferred_element_type=jnp.float32).astype(jnp.bfloat16)
        out[g] = (tiles[g].astype(jnp.float32) - template.astype(jnp.float32)).astype(out.dtype)


def subtract(tiles, rings, routes, coadd, group):
    count, side, _ = tiles.shape
    return pl.pallas_call(
        match_kernel,
        grid_spec=pltpu.PrefetchScalarGridSpec(
            num_scalar_prefetch=1,
            grid=(count // group,),
            in_specs=[
                pl.BlockSpec((group, 2, 128), lambda i, *_: (i, 0, 0)),
                pl.BlockSpec((group, side, side), lambda i, *_: (i, 0, 0)),
                pl.BlockSpec(coadd.shape, lambda i, *_: (0, 0, 0)),
            ],
            out_specs=pl.BlockSpec((group, side, side), lambda i, *_: (i, 0, 0)),
        ),
        out_shape=jax.ShapeDtypeStruct(tiles.shape, jnp.bfloat16),
        name="subtract",
    )(routes, rings, tiles, coadd)


def ring_rows(taps):
    count, _, kernel = taps.shape
    both = jnp.stack([taps[:, 0, :], taps[:, 1, ::-1]], axis=1).astype(jnp.float32)
    reach = kernel // 2
    gap = jnp.zeros((count, 2, 128 - kernel), jnp.float32)
    return jnp.concatenate([both[:, :, reach:], gap, both[:, :, :reach]], axis=2)


def local(warped_tiles, tile_weights, kernel_taps, patch_routes):
    patches = lax.axis_size("patch")
    side = warped_tiles.shape[1]
    routes = patch_routes[:, 0]
    weights = tile_weights.astype(jnp.float32)
    rings = ring_rows(kernel_taps)
    part, totals = local_sums(warped_tiles, weights, routes, patches, 64, jnp.float32)
    total = lax.psum(totals, ("visit", "patch"))
    mine = lax.psum_scatter(part, "patch", scatter_dimension=0, tiled=True)
    mine = lax.psum(mine, "visit")[0]
    own_total = lax.dynamic_index_in_dim(total, lax.axis_index("patch"), 0, keepdims=False)[0, 0]
    coadd_image = (mine / own_total).astype(jnp.bfloat16)[None]
    coadd = lax.all_gather(coadd_image, "patch", axis=0, tiled=True)
    difference = subtract(warped_tiles, rings, routes, coadd, 4)
    return (difference, coadd_image)


def solution(mesh):
    in_specs = (
        P(("visit", "patch"), None, None),
        P(("visit", "patch")),
        P(("visit", "patch"), None, None),
        P(("visit", "patch"), None),
    )
    out_specs = (P(("visit", "patch"), None, None), P("patch", None, None))
    return jax.shard_map(local, mesh=mesh, in_specs=in_specs, out_specs=out_specs, check_vma=False)
```

profile of v0, /device:TPU:0, one launch (start us, length us, event | category | flops | bytes accessed | tf_op | source)
XLA Modules:
  0.0 141.3 jit_solution(726925901417374998)
XLA Ops:
  7.2 0.0 copy-start
  7.2 0.0 reduce-scatter.2.cloned.1.call-start
  7.2 1.2 convert_element_type.11.weights
  8.4 5.6 %local_sums.1 = (f32[8,256,256]{2,1,0:T(8,128)}, f32[8,8,128]{2,1,0:T(8,128)}) custom-call(s32[32]{0:T(128)} %bitcast.4, f32[32]{0:T(128)} %convert_element_type.11.weights, bf16[32,256,256]{2,1,0:T(8,128)(2,1)} %tiles.3), custom_call_target="tpu_custom_call" | custom-call | tf_op jit(solution)/shard_map/local_sums/pallas_call | solution.py:25
  14.1 0.0 reduce-scatter.2.cloned.1.call-update
  14.1 0.0 all-reduce.2.cloned.1.call-start
  14.1 43.9 %reduce-scatter.2.cloned.1.call-done = f32[1,256,256]{2,1,0:T(8,128)} async-done(((f32[8,256,256]{2,1,0:T(8,128)}), f32[1,256,256]{2,1,0:T(8,128)}) %reduce-scatter.2.cloned.1.call-update) | async-done | bytes 262160 | tf_op jit(solution)/shard_map/reduce_scatter | solution.py:103
  58.1 0.0 all-reduce.2.cloned.1.call-update
  58.1 0.0 all-gather.2.cloned.1.call-start
  58.2 39.6 %psum.15 = f32[8,8,128]{2,1,0:T(8,128)S(1)} all-reduce(f32[8,8,128]{2,1,0:T(8,128)} %get-tuple-element.5), channel_id=1, replica_groups=mesh['visit'=4,'patch'=8] {'visit','patch'}, use_global_device_ids=true, to_apply=%region_2.0 | all-reduce | flops 8192 | bytes 65536 | tf_op jit(solution)/shard_map/psum | solution.py:102
  97.8 0.5 slice.19
  98.3 0.0 all-reduce.2.cloned.1.call-done
  98.3 2.3 %divide_convert_fusion = bf16[1,256,256]{2,1,0:T(8,128)(2,1)} fusion(f32[1,256,256]{2,1,0:T(8,128)} %all-reduce.2.cloned.1.call-done, f32[]{:T(128)} %bitcast.2), kind=kLoop, calls=%fused_computation | loop fusion | flops 131072 | bytes 393220 | tf_op jit(solution)/shard_map/convert_element_type | solution.py:106
  100.6 0.0 all-gather.2.cloned.1.call-update
  100.6 0.0 copy-done
  100.8 0.1 copy.10
  100.8 0.1 copy.9
  101.0 0.1 pad.1.clone
  101.0 0.7 pad_maximum_fusion.taps
  101.8 23.4 %all-gather.2.cloned.1.call-done.coadd = bf16[8,256,256]{2,1,0:T(8,128)(2,1)} async-done(((bf16[1,256,256]{2,1,0:T(8,128)(2,1)}), bf16[8,256,256]{2,1,0:T(8,128)(2,1)}) %all-gather.2.cloned.1.call-update) | async-done | bytes 1048592 | tf_op jit(solution)/shard_map/all_gather | solution.py:107
  125.1 9.6 %subtract.1 = bf16[32,256,256]{2,1,0:T(8,128)(2,1)} custom-call(s32[32]{0:T(128)} %bitcast.5, f32[32,2,128]{2,1,0:T(2,128)} %pad_maximum_fusion.taps, bf16[32,256,256]{2,1,0:T(8,128)(2,1)} %tiles.3, bf16[8,256,256]{2,1,0:T(8,128)(2,1)} %all-gather.2.cloned.1.call-done.coadd), custom_call_target="tpu_custom_call" | custom-call | tf_op jit(solution)/shard_map/subtract/pallas_call | solution.py:70
  (7 shorter events, 0.1 us)
Async XLA Ops:
  7.2 93.5 %copy-start = (bf16[32,2,15]{0,1,2:T(2,128)(2,1)S(1)}, bf16[32,2,15]{0,1,2:T(2,128)(2,1)}, u32[]{:S(2)}) copy-start(bf16[32,2,15]{0,1,2:T(2,128)(2,1)} %param.6) | copy-start | bytes 5764
  7.2 50.9 %reduce-scatter.2.cloned.1.call-start = ((), (), s32[]{:S(2)}) async-start(), calls=%async_computation.1 | async-start | bytes 2359296 | tf_op jit(solution)/shard_map/reduce_scatter | solution.py:103
  14.1 84.3 %all-reduce.2.cloned.1.call-start = ((), (), s32[]{:S(2)}) async-start(), calls=%async_computation.2 | async-start | bytes 524288 | tf_op jit(solution)/shard_map/psum | solution.py:104
  58.1 67.0 %all-gather.2.cloned.1.call-start = ((), (), s32[]{:S(2)}) async-start(), calls=%async_computation.3 | async-start | bytes 1179648 | tf_op jit(solution)/shard_map/all_gather | solution.py:107
Sparse Core Ops, SparseCore 0:
  14.2 43.8 reduce-scatter.1
  60.4 35.7 all-reduce.1
  100.8 24.3 all-gather.1
where the time goes:
time: 142 us; the launch traced here: 141 us
  waiting for transfers between devices  67.4 us (47%)
  blocking collectives  39.6 us (28%)
  Pallas kernels  15.3 us (11%)
  between operations  13.8 us (10%)
  other arithmetic  4.21 us (3%)
    reduce_scatter x1, waiting for transfers between devices, local(): mine = lax.psum_scatter(part, 'patch', scatter_dimension=0, tiled=True)  43.9 us
    psum x1, blocking collectives, local(): total = lax.psum(totals, ('visit', 'patch'))  39.6 us
    all_gather x1, waiting for transfers between devices, local(): coadd = lax.all_gather(coadd_image, 'patch', axis=0, tiled=True)  23.4 us
    pallas_call x1, Pallas kernels, subtract(): pl.pallas_call(match_kernel, grid_spec=pltpu.PrefetchScalarGridSpec(num_s...  9.65 us
    pallas_call x1, Pallas kernels, local_sums(): pl.pallas_call(functools.partial(sum_kernel, patches), grid_spec=pltpu.Pr...  5.65 us
  transfers between devices with their start and end apart: 3, of which 2 were waited for; matrix products, arithmetic and copies ran while one was open for 1% of the time, Pallas kernels for 0%

commit v1 on v0

--- a/solution.py
+++ b/solution.py
@@ -92,19 +92,236 @@
     return jnp.concatenate([both[:, :, reach:], gap, both[:, :, :reach]], axis=2)
 
 
+def merge_kernel(chips, visits, part, totals, coadd, own, half, chip_sum, inbox, lane_sum, lane_in, mine,
+                 tot_in, tot_mid, tot_z, core_s, core_r, chip_s, chip_r, lane_s, lane_r,
+                 back_s, back_r, fan_s, fan_r, pair_s, pair_r, tot_s, tot_r, totz_s, totz_r):
+    v = lax.axis_index("visit")
+    p = lax.axis_index("patch")
+    k, c = p // 2, p % 2
+    patches = 2 * chips
+    side = part.shape[2]
+    rows = side // visits
+    sibling = 2 * k + 1 - c
+
+    def span(r):
+        return pl.ds(pl.multiple_of(r * rows, rows), rows)
+
+    def remote(src, dst, send, recv, visit, patch):
+        return pltpu.make_async_remote_copy(
+            src_ref=src, dst_ref=dst, send_sem=send, recv_sem=recv,
+            device_id=(visit, patch), device_id_type=pl.DeviceIdType.MESH)
+
+    def chip_at(o):
+        return lax.rem(k + o, chips)
+
+    def visit_at(o):
+        return lax.rem(v + o, visits)
+
+    def loop(low, high, body):
+        if (high - low) <= 4:
+            for i in range(low, high):
+                body(i)
+        else:
+            lax.fori_loop(low, high, lambda i, _: (body(i), 0)[1], 0)
+
+    def core_copy(j, r):
+        return remote(part.at[j, 1 - c, span(r)], half.at[j, span(r)], core_s.at[j, r], core_r.at[j, r], v, sibling)
+
+    def chip_copy(j, slot, r):
+        return remote(chip_sum.at[j, span(r)], inbox.at[slot, span(r)], chip_s.at[j, r], chip_r.at[slot, r], v, 2 * j + c)
+
+    def lane_copy(u, slot):
+        return remote(lane_sum.at[u], lane_in.at[slot], lane_s.at[u], lane_r.at[slot], u, p)
+
+    def tot_copy(q, slot):
+        return remote(totals.at[q], tot_in.at[slot], tot_s.at[q], tot_r.at[slot], v, q)
+
+    def totz_copy(u, slot):
+        return remote(tot_mid, tot_z.at[slot], totz_s.at[u], totz_r.at[slot], u, p)
+
+    def back_copy(u, r):
+        piece = coadd.at[p, span(r)]
+        return remote(piece, piece, back_s.at[u], back_r.at[r], u, p)
+
+    def fan_copy(j, slot, r):
+        piece = coadd.at[2 * slot + c, span(r)]
+        return remote(piece, piece, fan_s.at[j, r], fan_r.at[slot, r], v, 2 * j + c)
+
+    def pair_copy(j, core, r):
+        piece = coadd.at[2 * j + core, span(r)]
+        return remote(piece, piece, pair_s.at[j, r], pair_r.at[j, r], v, sibling)
+
+    barrier = pltpu.get_barrier_semaphore()
+
+    def greet_patch(o):
+        pl.semaphore_signal(barrier, inc=1, device_id=(v, lax.rem(p + o, patches)), device_id_type=pl.DeviceIdType.MESH)
+
+    def greet_visit(o):
+        pl.semaphore_signal(barrier, inc=1, device_id=(visit_at(o), p), device_id_type=pl.DeviceIdType.MESH)
+
+    loop(1, patches, greet_patch)
+    loop(1, visits, greet_visit)
+    pl.semaphore_wait(barrier, patches - 1 + visits - 1)
+
+    def start_core(i):
+        r = visit_at(i + 1)
+        loop(1, chips + 1, lambda o: core_copy(chip_at(o), r).start())
+
+    loop(0, visits, start_core)
+
+    def start_tot(o):
+        tot_copy(lax.rem(p + o, patches), p).start()
+
+    loop(1, patches, start_tot)
+
+    def send_chips(i):
+        r = visit_at(i + 1)
+
+        def one(o):
+            j = chip_at(o)
+            core_copy(j, r).wait_recv()
+            chip_sum[j, span(r)] = (
+                part[j, c, span(r)].astype(jnp.float32) + half[j, span(r)].astype(jnp.float32)
+            ).astype(jnp.bfloat16)
+            chip_copy(j, k, r).start()
+
+        loop(1, chips, one)
+
+    loop(0, visits, send_chips)
+
+    tot_mid[...] = totals[p]
+
+    def add_tot(o):
+        q = lax.rem(p + o, patches)
+        tot_copy(q, q).wait_recv()
+        tot_mid[...] += tot_in[q]
+
+    loop(1, patches, add_tot)
+    loop(1, visits, lambda o: totz_copy(visit_at(o), v).start())
+
+    def gather(r):
+        core_copy(k, r).wait_recv()
+        mine[...] = part[k, c, span(r)].astype(jnp.float32) + half[k, span(r)].astype(jnp.float32)
+
+        def one(o):
+            j = chip_at(o)
+            chip_copy(j, j, r).wait_recv()
+            mine[...] += inbox[j, span(r)].astype(jnp.float32)
+
+        loop(1, chips, one)
+
+    def send_lane(i):
+        r = visit_at(i)
+        gather(r)
+        lane_sum[r] = mine[...].astype(jnp.bfloat16)
+        lane_copy(r, v).start()
+
+    loop(1, visits, send_lane)
+    gather(v)
+    tot_z[v] = tot_mid[...]
+
+    def add_lane(o):
+        u = visit_at(o)
+        lane_copy(u, u).wait_recv()
+        mine[...] += lane_in[u].astype(jnp.float32)
+        totz_copy(u, u).wait_recv()
+        tot_z[v] += tot_z[u]
+
+    loop(1, visits, add_lane)
+    coadd[p, span(v)] = (mine[...] / tot_z[v][0:1, 0:1]).astype(jnp.bfloat16)
+
+    loop(1, visits, lambda o: back_copy(visit_at(o), v).start())
+
+    def fan_out(r):
+        loop(1, chips, lambda o: fan_copy(chip_at(o), k, r).start())
+        pair_copy(k, c, r).start()
+
+    def forward(r):
+        def one(o):
+            j = chip_at(o)
+            fan_copy(j, j, r).wait_recv()
+            pair_copy(j, c, r).start()
+
+        loop(1, chips, one)
+
+    fan_out(v)
+
+    def relay(i):
+        r = visit_at(i)
+        back_copy(r, r).wait_recv()
+        fan_out(r)
+        forward(visit_at(i - 1))
+
+    loop(1, visits, relay)
+    own[0] = coadd[p]
+    forward(visit_at(visits - 1))
+
+    def finish(i):
+        def one(o):
+            j = chip_at(o)
+            pair_copy(j, 1 - c, i).wait_recv()
+            pair_copy(j, c, i).wait_send()
+            core_copy(j, i).wait_send()
+
+        def peer(o):
+            j = chip_at(o)
+            chip_copy(j, k, i).wait_send()
+            fan_copy(j, k, i).wait_send()
+
+        loop(0, chips, one)
+        loop(1, chips, peer)
+
+    loop(0, visits, finish)
+
+    def finish_visit(o):
+        u = visit_at(o)
+        lane_copy(u, v).wait_send()
+        totz_copy(u, v).wait_send()
+        back_copy(u, v).wait_send()
+
+    loop(1, visits, finish_visit)
+    loop(1, patches, lambda o: tot_copy(lax.rem(p + o, patches), p).wait_send())
+
+
+def merge(part, totals, patches, visits):
+    side = part.shape[1]
+    chips = patches // 2
+    rows = side // visits
+    dma = pltpu.SemaphoreType.DMA
+    block = pl.BlockSpec(memory_space=pltpu.VMEM)
+    pairs = [dma((chips, visits))] * 2
+    return pl.pallas_call(
+        functools.partial(merge_kernel, chips, visits),
+        in_specs=[block, block],
+        out_specs=[block, block],
+        out_shape=[
+            jax.ShapeDtypeStruct((patches, side, side), jnp.bfloat16),
+            jax.ShapeDtypeStruct((1, side, side), jnp.bfloat16),
+        ],
+        scratch_shapes=[
+            pltpu.VMEM((chips, side, side), jnp.bfloat16),
+            pltpu.VMEM((chips, side, side), jnp.bfloat16),
+            pltpu.VMEM((chips, side, side), jnp.bfloat16),
+            pltpu.VMEM((visits, rows, side), jnp.bfloat16),
+            pltpu.VMEM((visits, rows, side), jnp.bfloat16),
+            pltpu.VMEM((rows, side), jnp.float32),
+            pltpu.VMEM((patches, 8, 128), jnp.float32),
+            pltpu.VMEM((8, 128), jnp.float32),
+            pltpu.VMEM((visits, 8, 128), jnp.float32),
+        ] + pairs + pairs + [dma((visits,))] * 4 + pairs + pairs + [dma((patches,))] * 2 + [dma((visits,))] * 2,
+        compiler_params=pltpu.CompilerParams(collective_id=0, has_side_effects=True),
+        name="merge",
+    )(part.reshape(chips, 2, side, side), totals)
+
+
 def local(warped_tiles, tile_weights, kernel_taps, patch_routes):
     patches = lax.axis_size("patch")
     side = warped_tiles.shape[1]
     routes = patch_routes[:, 0]
     weights = tile_weights.astype(jnp.float32)
     rings = ring_rows(kernel_taps)
-    part, totals = local_sums(warped_tiles, weights, routes, patches, 64, jnp.float32)
-    total = lax.psum(totals, ("visit", "patch"))
-    mine = lax.psum_scatter(part, "patch", scatter_dimension=0, tiled=True)
-    mine = lax.psum(mine, "visit")[0]
-    own_total = lax.dynamic_index_in_dim(total, lax.axis_index("patch"), 0, keepdims=False)[0, 0]
-    coadd_image = (mine / own_total).astype(jnp.bfloat16)[None]
-    coadd = lax.all_gather(coadd_image, "patch", axis=0, tiled=True)
+    part, totals = local_sums(warped_tiles, weights, routes, patches, 64, jnp.bfloat16)
+    coadd, coadd_image = merge(part, totals, patches, lax.axis_size("visit"))
     difference = subtract(warped_tiles, rings, routes, coadd, 4)
     return (difference, coadd_image)
 

time: 142 us -> 51.3 us (0.36)
  waiting for transfers between devices: 67.4 us -> 0 us
  blocking collectives: 39.6 us -> 0 us
  Pallas kernels: 15.3 us -> 45.9 us
  between operations: 13.8 us -> 0.68 us
  other arithmetic: 4.21 us -> 1.95 us
    reduce_scatter x1 -> x0, waiting for transfers between devices: 43.9 us -> none  [local(): mine = lax.psum_scatter(part, 'patch', scatter_dimension=0, tiled=True)]
    psum x1 -> x0, blocking collectives: 39.6 us -> none  [local(): total = lax.psum(totals, ('visit', 'patch'))]
    pallas_call x0 -> x1, Pallas kernels: none -> 30.7 us  [merge(): pl.pallas_call(functools.partial(merge_kernel, chips, visits), in_specs=[...]
    all_gather x1 -> x0, waiting for transfers between devices: 23.4 us -> none  [local(): coadd = lax.all_gather(coadd_image, 'patch', axis=0, tiled=True)]
    convert_element_type x1 -> x0, other arithmetic: 2.27 us -> none  [local(): coadd_image = (mine / own_total).astype(jnp.bfloat16)[None]]
  transfers between devices with their start and end apart: 3 -> 0, of which waited for: 2 -> 0; matrix products, arithmetic and copies ran while one was open for 1% -> 0% of each run, Pallas kernels for 0% -> 0%
where the time goes in v1:
time: 51.3 us; the launch traced here: 50.3 us
  Pallas kernels  45.9 us (89%)
  other arithmetic  1.95 us (4%)
  local copies, waits for them, and re-layouts  1.74 us (3%)
  between operations  0.68 us (1%)
    pallas_call x1, Pallas kernels, merge(): pl.pallas_call(functools.partial(merge_kernel, chips, visits), in_specs=[...  30.7 us
    pallas_call x1, Pallas kernels, subtract(): pl.pallas_call(match_kernel, grid_spec=pltpu.PrefetchScalarGridSpec(num_s...  9.83 us
    pallas_call x1, Pallas kernels, local_sums(): pl.pallas_call(functools.partial(sum_kernel, patches), grid_spec=pltpu.Pr...  5.45 us
    convert_element_type x1, other arithmetic, local(): weights = tile_weights.astype(jnp.float32)  1.2 us

profile of v1, /device:TPU:0, one launch (start us, length us, event | category | flops | bytes accessed | tf_op | source)
XLA Modules:
  0.0 50.3 jit_solution(14744251836235146904)
XLA Ops:
  0.6 1.2 %convert_element_type.7.weights = f32[32]{0:T(128)} convert(bf16[32]{0:T(256)(128)(2,1)} %param.5) | non-fusion elementwise | flops 32 | bytes 192 | tf_op jit(solution)/shard_map/convert_element_type | solution.py:321
  1.8 0.1 pad.1.clone
  1.9 0.8 %fusion = (bf16[32,1,15]{0,1,2:T(2,128)(2,1)S(1)}, bf16[32,1,15]{0,1,2:T(2,128)(2,1)S(1)}) fusion(bf16[32,2,15]{0,1,2:T(2,128)(2,1)} %param.6), kind=kLoop, calls=%fused_computation.2 | loop fusion | bytes 3840 | tf_op jit(solution)/shard_map/slice | solution.py:89
  2.8 0.1 copy.10
  2.9 0.1 copy.9
  3.0 0.7 %pad_maximum_fusion.taps = f32[32,2,128]{2,1,0:T(2,128)} fusion(f32[32,2,7]{2,1,0:T(2,128)S(1)} %copy.9, f32[32,2,8]{2,1,0:T(2,128)S(1)} %copy.10, f32[128]{0:T(128)S(1)} %pad.1.clone), kind=kLoop, calls=%fused_computation | loop fusion | flops 16384 | bytes 37120 | tf_op jit(solution)/shard_map/concatenate | solution.py:92
  3.7 5.4 %local_sums.1 = (bf16[8,256,256]{2,1,0:T(8,128)(2,1)}, f32[8,8,128]{2,1,0:T(8,128)}) custom-call(s32[32]{0:T(128)} %bitcast.3, f32[32]{0:T(128)} %convert_element_type.7.weights, bf16[32,256,256]{2,1,0:T(8,128)(2,1)} %tiles.3), custom_call_target="tpu_custom_call" | custom-call | tf_op jit(solution)/shard_map/local_sums/pallas_call | solution.py:25
  9.1 30.7 %merge.1 = (bf16[8,256,256]{2,1,0:T(8,128)(2,1)}, bf16[1,256,256]{2,1,0:T(8,128)(2,1)}) custom-call(bf16[4,2,256,256]{3,2,1,0:T(8,128)(2,1)} %bitcast.2, f32[8,8,128]{2,1,0:T(8,128)} %get-tuple-element.7.totals), custom_call_target="tpu_custom_call" | custom-call | tf_op jit(solution)/shard_map/merge/pallas_call | solution.py:293
  39.8 0.0 copy-start
  39.8 9.8 %subtract.1 = bf16[32,256,256]{2,1,0:T(8,128)(2,1)} custom-call(s32[32]{0:T(128)} %bitcast.4, f32[32,2,128]{2,1,0:T(2,128)} %pad_maximum_fusion.taps, bf16[32,256,256]{2,1,0:T(8,128)(2,1)} %tiles.3, bf16[8,256,256]{2,1,0:T(8,128)(2,1)} %get-tuple-element.8.coadd), custom_call_target="tpu_custom_call" | custom-call | tf_op jit(solution)/shard_map/subtract/pallas_call | solution.py:70
  49.7 0.0 copy-done
  49.7 0.7 %copy.12 = bf16[1,256,256]{2,1,0:T(8,128)(2,1)} copy(bf16[1,256,256]{2,1,0:T(8,128)(2,1)S(1)} %copy-done) | data formatting | bytes 262144
  (5 shorter events, 0.0 us)
Async XLA Ops:
  39.8 9.8 %copy-start = (bf16[1,256,256]{2,1,0:T(8,128)(2,1)S(1)}, bf16[1,256,256]{2,1,0:T(8,128)(2,1)}, u32[]{:S(2)}) copy-start(bf16[1,256,256]{2,1,0:T(8,128)(2,1)} %get-tuple-element.15) | copy-start | bytes 393220
